TPU v7x, 32 devices: a whole 2x2x4 slice. The times are simulated.
32 devices in a mesh: dp: 4 (over y, x), tensor: 8 (over z, core).
Axes of the slice: x: 2, y: 2, z: 4, core: 2. Of those that a mesh axis runs over, the one named last changes fastest.
Arguments:
- tokens: bfloat16 [8, 256, 8192], P('dp'), may hold values from -6 to 6
- segments: int32 [8, 256], P('dp'), may hold values from 0 to 3, never falling along the last dimension, each value on 1 to 128 neighbouring positions
- norm_gain: float32 [8192], replicated, may hold values from 0.25 to 3.5
- q_weight: bfloat16 [8192, 4096], P('dp', 'tensor'), may hold values from -1.3479223 to 1.3479223
- kv_weight: bfloat16 [2, 8192, 512], P(None, 'dp'), may hold values from -0.055242717 to 0.055242717
- o_weight: bfloat16 [4096, 8192], P('tensor', 'dp'), may hold values from -0.09375 to 0.09375
- basis_query: bfloat16 [8, 8192, 4096], P(None, 'dp', 'tensor'), may hold values from -11 to 11
- basis_output: bfloat16 [8, 4096, 8192], P(None, 'tensor', 'dp'), may hold values from -11 to 11
Outputs:
- next_query: bfloat16 [8192, 4096], P('dp', 'tensor')
- next_output: bfloat16 [4096, 8192], P('tensor', 'dp')
- coefficients: float32 [9], replicated
Inputs may be any that keep to these rules, and one draw needn't show every extreme that they name: `segments`: segment numbers never fall along a sequence.
All inputs are finite; a program needn't handle non-finite values.
Results may differ from a plain program's by a relative error of at most 0.018.
Values may be sent and summed in bfloat16 or wider, within the bound.
No kernel may reach another device: no remote copies, remote signals or barrier semaphores. Data moves between devices by JAX's collectives and lax.ppermute only.
A program may use at most 192 MiB of HBM per device.

v0:
```python
import math
import jax
import jax.numpy as jnp
from jax import lax
from jax.sharding import PartitionSpec as P

D = 8192
HD = 128
QH = 32
KVH = 4
K = 8
PRECISE = lax.Precision.HIGHEST
ROPE_BASE = 500000.0
NORM_EPS = 1e-05
BETA_EPS = 1e-06


def rope_tables(length, head_width):
    half_width = head_width // 2
    frequency = jnp.exp(
        jnp.arange(half_width, dtype=jnp.float32) * (-2.0 * math.log(ROPE_BASE) / head_width)
    )
    angles = jnp.arange(length, dtype=jnp.float32)[:, None] * frequency[None, :]
    return (jnp.cos(angles), jnp.sin(angles))


def rotate(vectors, cosine_table, sine_table):
    half_width = vectors.shape[-1] // 2
    front_half = vectors[..., :half_width]
    back_half = vectors[..., half_width:]
    return jnp.concatenate(
        [
            front_half * cosine_table - back_half * sine_table,
            front_half * sine_table + back_half * cosine_table,
        ],
        axis=-1,
    )


def attend(query, key_states, values, allowed):
    length = query.shape[1]
    head_width = query.shape[-1]
    cosine_table, sine_table = rope_tables(length, head_width)
    query = rotate(query, cosine_table[:, None, :], sine_table[:, None, :])
    key_states = rotate(key_states, cosine_table, sine_table)
    scores = jnp.einsum("slgd,smd->sglm", query, key_states, precision=PRECISE) * head_width ** (
        -0.5
    )
    scores = jnp.where(allowed[:, None, :, :], scores, -1e30)
    row_max = lax.stop_gradient(jnp.max(scores, axis=-1, keepdims=True))
    weights = jnp.exp(scores - row_max)
    probabilities = weights / jnp.sum(weights, axis=-1, keepdims=True)
    return jnp.einsum("sglm,smd->slgd", probabilities, values, precision=PRECISE)


def allowed_pairs(segments):
    length = segments.shape[1]
    position = jnp.arange(length, dtype=jnp.int32)
    causal = position[:, None] >= position[None, :]
    return jnp.logical_and(segments[:, :, None] == segments[:, None, :], causal[None])


def rms_normed(tokens, norm_gain):
    flat_rows = tokens.reshape(-1, tokens.shape[-1]).astype(jnp.float32)
    inv_rms = lax.rsqrt(jnp.mean(flat_rows * flat_rows, axis=1, keepdims=True) + NORM_EPS)
    return (flat_rows * inv_rms * norm_gain[None, :]).astype(jnp.bfloat16)


def block_products(left_rows, right_rows, block_count, factor):
    left_blocks = left_rows.reshape(block_count, -1, left_rows.shape[1])
    right_blocks = right_rows.reshape(block_count, -1, right_rows.shape[1])
    terms = (
        jnp.einsum("nta,ntb->nab", left_blocks, right_blocks, preferred_element_type=jnp.float32)
        * factor
    )
    rounded = lax.optimization_barrier(terms.astype(jnp.bfloat16))
    return jnp.sum(rounded.astype(jnp.float32), axis=0)


def body(tokens, segments, norm_gain, q_weight, kv_weight, o_weight, basis_query, basis_output):
    groups = lax.axis_size("dp")
    seq_count, length, model_width = tokens.shape
    row_count = seq_count * length
    col_count = q_weight.shape[1]
    heads_dev = col_count // HD
    group_size = QH // KVH
    qwidth = QH * HD
    query_scale = D ** (-0.5)
    output_scale = qwidth ** (-0.5)
    gn_scale = qwidth / (row_count * groups)
    param_count = 2.0 * D * qwidth
    normed = rms_normed(tokens, norm_gain)
    dir_query = basis_query[K - 1]
    dir_output = basis_output[K - 1]
    kv_head = lax.axis_index("tensor") * heads_dev // group_size
    kv_columns = lax.dynamic_slice_in_dim(kv_weight, kv_head * HD, HD, 2)
    kv_pair = jnp.concatenate([kv_columns[0], kv_columns[1]], axis=1)
    sum_query = jnp.dot(
        normed,
        lax.all_gather(q_weight, "dp", axis=0, tiled=True),
        preferred_element_type=jnp.float32,
    )
    sum_tangent = jnp.dot(
        normed,
        lax.all_gather(dir_query, "dp", axis=0, tiled=True),
        preferred_element_type=jnp.float32,
    )
    sum_pair = jnp.dot(
        normed,
        lax.all_gather(kv_pair, "dp", axis=0, tiled=True),
        preferred_element_type=jnp.float32,
    )
    query = sum_query.astype(jnp.bfloat16)
    tangent = (sum_tangent * query_scale).astype(jnp.bfloat16)
    key_states = sum_pair[:, :HD].astype(jnp.bfloat16)
    values = sum_pair[:, HD:].astype(jnp.bfloat16)
    allowed = allowed_pairs(segments)
    query_wide = query.astype(jnp.float32).reshape(seq_count, length, heads_dev, HD)
    tangent_wide = tangent.astype(jnp.float32).reshape(seq_count, length, heads_dev, HD)
    key_wide = key_states.astype(jnp.float32).reshape(seq_count, length, HD)
    value_wide = values.astype(jnp.float32).reshape(seq_count, length, HD)

    def attend_here(moving):
        return attend(moving, key_wide, value_wide, allowed)

    heads_out, tangent_heads = jax.jvp(attend_here, (query_wide,), (tangent_wide,))
    heads_out = heads_out.reshape(row_count, col_count).astype(jnp.bfloat16)
    tangent_heads = tangent_heads.reshape(row_count, col_count).astype(jnp.bfloat16)
    all_heads, all_tangent = (
        lax.all_gather(heads_out, "dp", axis=0, tiled=True),
        lax.all_gather(tangent_heads, "dp", axis=0, tiled=True),
    )
    group_term = jnp.dot(
        all_heads, dir_output, preferred_element_type=jnp.float32
    ) * output_scale + jnp.dot(all_tangent, o_weight, preferred_element_type=jnp.float32)
    tangent_columns = lax.psum(group_term.astype(jnp.bfloat16), "tensor")
    cot_heads = lax.psum_scatter(
        lax.dot_general(
            tangent_columns, o_weight, (((1,), (1,)), ((), ())), preferred_element_type=jnp.float32
        ).astype(jnp.bfloat16),
        "dp",
        scatter_dimension=0,
        tiled=True,
    ).astype(jnp.float32)
    gn_output = block_products(all_heads, tangent_columns, groups, gn_scale * output_scale)
    _, pullback = jax.vjp(attend_here, query_wide)
    cot_query = pullback(cot_heads.reshape(seq_count, length, heads_dev, HD))[0]
    cot_query = cot_query.reshape(row_count, col_count).astype(jnp.bfloat16)
    gn_query = lax.psum_scatter(
        (
            lax.dot_general(
                normed, cot_query, (((0,), (0,)), ((), ())), preferred_element_type=jnp.float32
            )
            * (gn_scale * query_scale)
        ).astype(jnp.bfloat16),
        "dp",
        scatter_dimension=0,
        tiled=True,
    ).astype(jnp.float32)

    def local_products(vec_query, vec_output):
        return jnp.sum(basis_query.astype(jnp.float32) * vec_query[None], axis=(1, 2)) + jnp.sum(
            basis_output.astype(jnp.float32) * vec_output[None], axis=(1, 2)
        )

    def remove(vec_query, vec_output, weights_now):
        return (
            vec_query
            - jnp.sum(weights_now[:, None, None] * basis_query.astype(jnp.float32), axis=0),
            vec_output
            - jnp.sum(weights_now[:, None, None] * basis_output.astype(jnp.float32), axis=0),
        )

    first_coeffs = lax.psum(local_products(gn_query, gn_output), ("dp", "tensor")) / param_count
    kept_query, kept_output = remove(gn_query, gn_output, first_coeffs)
    second_coeffs = (
        lax.psum(local_products(kept_query, kept_output), ("dp", "tensor")) / param_count
    )
    clean_query, clean_output = remove(kept_query, kept_output, second_coeffs)
    local_squares = jnp.sum(clean_query * clean_query) + jnp.sum(clean_output * clean_output)
    squares = lax.psum(local_squares, ("dp", "tensor")) / param_count
    beta = jnp.sqrt(squares + BETA_EPS)
    coefficients = jnp.concatenate([first_coeffs + second_coeffs, beta[None]])
    return (
        (clean_query / beta).astype(jnp.bfloat16),
        (clean_output / beta).astype(jnp.bfloat16),
        coefficients,
    )


def solution(mesh):
    return jax.shard_map(
        body,
        mesh=mesh,
        in_specs=(
            P("dp", None, None),
            P("dp", None),
            P(),
            P("dp", "tensor"),
            P(None, "dp", None),
            P("tensor", "dp"),
            P(None, "dp", "tensor"),
            P(None, "tensor", "dp"),
        ),
        out_specs=(P("dp", "tensor"), P("tensor", "dp"), P()),
        check_vma=False,
    )
```

profile of v0, /device:TPU:0, one launch (start us, length us, event | category | flops | bytes accessed | tf_op | source)
XLA Modules:
  0.0 907.9 jit_solution(18411011487311448735)
XLA Ops:
  13.7 5.1 multiply_reduce_fusion
  21.0 10.2 %fusion.9 = bf16[512,8192]{1,0:T(8,128)(2,1)} fusion(f32[8192]{0:T(1024)S(1)} %copy-done.18, f32[512]{0:T(512)S(1)} %bitcast.158, bf16[2,256,8192]{2,1,0:T(8,128)(2,1)} %param.8), kind=kLoop, calls=%fused_computation.18 | loop fusion | flops 16777216 | bytes 16812032 | tf_op jit(solution)/shard_map/convert_element_type | solution.py:66
  31.2 34.5 %all-gather.7.cloned.1.call-done = bf16[8192,256]{1,0:T(8,128)(2,1)} async-done(((bf16[2048,256]{1,0:T(8,128)(2,1)}), bf16[8192,256]{1,0:T(8,128)(2,1)}) %all-gather.7.cloned.1.call-update) | async-done | bytes 4194320 | tf_op jit(solution)/shard_map/all_gather | solution.py:110
  65.7 6.9 convolution_convert_fusion.2
  74.2 81.5 %all-gather.15.cloned.1.call-done = bf16[1,8192,512]{2,1,0:T(8,128)(2,1)} async-done(((bf16[1,2048,512]{2,1,0:T(8,128)(2,1)}), bf16[1,8192,512]{2,1,0:T(8,128)(2,1)}) %all-gather.15.cloned.1.call-update) | async-done | bytes 8388624 | tf_op jit(solution)/shard_map/all_gather | solution.py:105
  155.7 11.2 %fusion.44 = f32[512,512]{1,0:T(8,128)} fusion(bf16[512,8192]{1,0:T(8,128)(2,1)} %fusion.9, bf16[1,8192,512]{2,1,0:T(8,128)(2,1)} %all-gather.15.cloned.1.call-done), kind=kOutput, calls=%fused_computation.59 | convolution fusion | flops 4295753728 | bytes 17825792 | tf_op jit(solution)/shard_map/dot_general | solution.py:103
  168.5 76.5 %all-gather.9.cloned.1.call-done = bf16[8192,512]{1,0:T(8,128)(2,1)} async-done(((bf16[2048,512]{1,0:T(8,128)(2,1)}), bf16[8192,512]{1,0:T(8,128)(2,1)}) %all-gather.9.cloned.1.call-update) | async-done | bytes 8388624 | tf_op jit(solution)/shard_map/all_gather | solution.py:100
  245.0 11.4 %fusion.47 = f32[512,512]{1,0:T(8,128)} fusion(bf16[512,8192]{1,0:T(8,128)(2,1)} %fusion.9, bf16[8192,512]{1,0:T(8,128)(2,1)} %all-gather.9.cloned.1.call-done), kind=kOutput, calls=%fused_computation.61 | convolution fusion | flops 4295491584 | bytes 17825792 | tf_op jit(solution)/shard_map/dot_general | solution.py:98
  279.6 28.8 %all-gather.13.cloned.1.call-done = bf16[2048,512]{1,0:T(8,128)(2,1)} async-done(((bf16[512,512]{1,0:T(8,128)(2,1)}), bf16[2048,512]{1,0:T(8,128)(2,1)}) %all-gather.13.cloned.1.call-update) | async-done | bytes 2097168 | tf_op jit(solution)/shard_map/all_gather | solution.py:131
  308.5 9.9 %fusion.95 = f32[2048,2048]{1,0:T(8,128)} fusion(bf16[2048,512]{1,0:T(8,128)(2,1)} %all-gather.13.cloned.1.call-done, bf16[512,2048]{1,0:T(8,128)(2,1)S(1)} %copy-done), kind=kOutput, calls=%fused_computation.134 | convolution fusion | flops 4294967296 | bytes 20971520 | tf_op jit(solution)/shard_map/dot_general | solution.py:135
  318.4 27.0 %all-gather.11.cloned.1.call-done = bf16[2048,512]{1,0:T(8,128)(2,1)} async-done(((bf16[512,512]{1,0:T(8,128)(2,1)}), bf16[2048,512]{1,0:T(8,128)(2,1)}) %all-gather.11.cloned.1.call-update) | async-done | bytes 2097168 | tf_op jit(solution)/shard_map/all_gather | solution.py:130
  345.4 14.8 %add_convert_fusion = bf16[2048,2048]{1,0:T(8,128)(2,1)} fusion(f32[2048,2048]{1,0:T(8,128)} %fusion.95, bf16[2048,512]{1,0:T(8,128)(2,1)} %all-gather.11.cloned.1.call-done, bf16[8,512,2048]{2,1,0:T(8,128)(2,1)} %param.15), kind=kOutput, calls=%fused_computation.22 | convolution fusion | flops 4307550208 | bytes 29360128 | tf_op jit(solution)/shard_map/dot_general | solution.py:133
  360.3 175.6 %all-reduce.4.cloned.1.call-done = bf16[2048,2048]{1,0:T(8,128)(2,1)} async-done(((bf16[2048,2048]{1,0:T(8,128)(2,1)}), bf16[2048,2048]{1,0:T(8,128)(2,1)}) %all-reduce.4.cloned.1.call-update) | async-done | bytes 8388624 | tf_op jit(solution)/shard_map/psum | solution.py:136
  535.9 9.1 %convolution_convert_fusion = bf16[2048,512]{1,0:T(8,128)(2,1)} fusion(bf16[2048,2048]{1,0:T(8,128)(2,1)} %all-reduce.4.cloned.1.call-done, bf16[512,2048]{1,0:T(8,128)(2,1)S(1)} %copy-done), kind=kOutput, calls=%fused_computation.31 | convolution fusion | flops 4296015872 | bytes 12582912 | tf_op jit(solution)/shard_map/dot_general | solution.py:138
  546.2 10.0 %multiply_convert_fusion.2 = bf16[2,256,8192]{2,1,0:T(8,128)(2,1)} fusion(f32[8192]{0:T(1024)S(1)} %copy-done.19, f32[2,256]{1,0:T(2,128)S(1)} %copy-done.23, bf16[2,256,8192]{2,1,0:T(8,128)(2,1)} %param.8), kind=kLoop, calls=%fused_computation.23 | loop fusion | flops 16777216 | bytes 16812032 | tf_op jit(solution)/shard_map/convert_element_type | solution.py:66
  556.2 24.3 %reduce-scatter.3.cloned.1.call-done = bf16[512,512]{1,0:T(8,128)(2,1)} async-done(((bf16[2048,512]{1,0:T(8,128)(2,1)}), bf16[512,512]{1,0:T(8,128)(2,1)}) %reduce-scatter.3.cloned.1.call-update) | async-done | bytes 524304 | tf_op jit(solution)/shard_map/reduce_scatter | solution.py:137
  590.7 7.1 multiply_convert_fusion.1
  599.4 10.3 %multiply_convert_fusion = bf16[4,512,2048]{2,1,0:T(8,128)(2,1)} fusion(bf16[4,512,512]{2,1,0:T(8,128)(2,1)S(1)} %bitcast.160, bf16[4,512,2048]{2,1,0:T(8,128)(2,1)} %bitcast.159), kind=kOutput, calls=%fused_computation.20 | convolution fusion | flops 4303355904 | bytes 18874368 | tf_op jit(solution)/shard_map/nta,ntb->nab/dot_general | solution.py:73
  609.7 5.9 convert_reduce_fusion
  617.6 7.8 fusion.4
  625.4 58.9 %reduce-scatter.5.cloned.1.call-done = bf16[2048,512]{1,0:T(8,128)(2,1)} async-done(((bf16[8192,512]{1,0:T(8,128)(2,1)}), bf16[2048,512]{1,0:T(8,128)(2,1)}) %reduce-scatter.5.cloned.1.call-update) | async-done | bytes 2097168 | tf_op jit(solution)/shard_map/reduce_scatter | solution.py:149
  686.5 8.0 fusion
  694.5 39.5 %psum.29 = f32[8]{0:T(128)S(1)} all-reduce(f32[8]{0:T(128)S(1)} %add.69), channel_id=1, replica_groups=mesh['dp'=4,'tensor'=8] {'dp','tensor'}, use_global_device_ids=true, to_apply=%region_11.12 | all-reduce | flops 8 | bytes 64 | tf_op jit(solution)/shard_map/psum | solution.py:174
  734.0 11.9 %fusion.5 = f32[512,2048]{1,0:T(8,128)S(1)} fusion(bf16[8,512,2048]{2,1,0:T(8,128)(2,1)} %param.15, f32[8]{0:T(128)S(1)} %broadcast_multiply_fusion.1), kind=kLoop, calls=%fused_computation.13 | loop fusion | flops 24117248 | bytes 20971552 | tf_op jit(solution)/shard_map/reduce_sum | solution.py:171
  746.0 14.8 %fusion.1 = f32[2048,512]{1,0:T(8,128)} fusion(bf16[8,2048,512]{2,1,0:T(8,128)(2,1)} %param.14, f32[8]{0:T(128)S(1)} %broadcast_multiply_fusion.1), kind=kLoop, calls=%fused_computation.9 | loop fusion | flops 24117248 | bytes 20971552 | tf_op jit(solution)/shard_map/reduce_sum | solution.py:169
  764.2 7.6 fusion.6
  775.2 5.4 fusion.2
  780.6 40.9 %psum.30 = f32[8]{0:T(128)S(1)} all-reduce(f32[8]{0:T(128)S(1)} %add.70), channel_id=1, replica_groups=mesh['dp'=4,'tensor'=8] {'dp','tensor'}, use_global_device_ids=true, to_apply=%region_16.17 | all-reduce | flops 8 | bytes 64 | tf_op jit(solution)/shard_map/psum | solution.py:177
  821.5 11.9 %fusion.7 = f32[512,2048]{1,0:T(8,128)S(1)} fusion(bf16[8,512,2048]{2,1,0:T(8,128)(2,1)} %param.15, f32[8]{0:T(128)S(1)} %get-tuple-element.32), kind=kLoop, calls=%fused_computation.15 | loop fusion | flops 24117248 | bytes 20971552 | tf_op jit(solution)/shard_map/reduce_sum | solution.py:171
  833.5 12.1 %fusion.3 = f32[2048,512]{1,0:T(8,128)S(1)} fusion(bf16[8,2048,512]{2,1,0:T(8,128)(2,1)} %param.14, f32[8]{0:T(128)S(1)} %get-tuple-element.32), kind=kLoop, calls=%fused_computation.11 | loop fusion | flops 24117248 | bytes 20971552 | tf_op jit(solution)/shard_map/reduce_sum | solution.py:169
  854.2 39.1 %psum.31 = f32[]{:T(128)} all-reduce(f32[]{:T(128)S(6)} %add.71), channel_id=1, replica_groups=mesh['dp'=4,'tensor'=8] {'dp','tensor'}, use_global_device_ids=true, to_apply=%region_21.22 | all-reduce | flops 1 | bytes 8 | tf_op jit(solution)/shard_map/psum | solution.py:181
  894.0 4.1 divide_convert_fusion
  (135 shorter events, 68.5 us)
Async XLA Ops:
  7.2 301.3 %copy-start = (bf16[512,2048]{1,0:T(8,128)(2,1)S(1)}, bf16[512,2048]{1,0:T(8,128)(2,1)}, u32[]{:S(2)}) copy-start(bf16[512,2048]{1,0:T(8,128)(2,1)} %param.13) | copy-start | bytes 6291460
  7.2 58.6 %all-gather.7.cloned.1.call-start = ((), (), s32[]{:S(2)}) async-start(), calls=%async_computation.2 | async-start | bytes 5242880 | tf_op jit(solution)/shard_map/all_gather | solution.py:110
  9.8 145.9 %all-gather.15.cloned.1.call-start = ((), (), s32[]{:S(2)}) async-start(), calls=%async_computation.9 | async-start | bytes 10485760 | tf_op jit(solution)/shard_map/all_gather | solution.py:105
  12.9 232.1 %all-gather.9.cloned.1.call-start = ((), (), s32[]{:S(2)}) async-start(), calls=%async_computation.3 | async-start | bytes 10485760 | tf_op jit(solution)/shard_map/all_gather | solution.py:100
  13.6 6.3 copy-start.22
  13.7 7.3 copy-start.18
  13.7 294.8 %all-gather.13.cloned.1.call-start = ((), (), s32[]{:S(2)}) async-start(), calls=%async_computation.5 | async-start | bytes 2621440 | tf_op jit(solution)/shard_map/all_gather | solution.py:131
  20.0 53.4 %copy-start.12 = (f32[256,64]{1,0:T(8,128)}, f32[256,64]{1,0:T(8,128)S(1)}, u32[]{:S(2)}) copy-start(f32[256,64]{1,0:T(8,128)S(1)} %get-tuple-element.34) | copy-start | bytes 196612
  273.2 72.2 %all-gather.11.cloned.1.call-start = ((), (), s32[]{:S(2)}) async-start(), calls=%async_computation.4 | async-start | bytes 2621440 | tf_op jit(solution)/shard_map/all_gather | solution.py:130
  279.6 256.3 %all-reduce.4.cloned.1.call-start = ((), (), s32[]{:S(2)}) async-start(), calls=%async_computation.6 | async-start | bytes 16777216 | tf_op jit(solution)/shard_map/psum | solution.py:136
  360.2 185.1 %copy-start.16 = (pred[2,256,256]{1,2,0:T(8,128)(4,1)S(1)}, pred[2,256,256]{1,2,0:T(8,128)(4,1)}, u32[]{:S(2)}) copy-start(pred[2,256,256]{1,2,0:T(8,128)(4,1)} %get-tuple-element.27) | copy-start | bytes 393220
  360.2 185.9 %copy-start.19 = (f32[8192]{0:T(1024)S(1)}, f32[8192]{0:T(1024)}, u32[]{:S(2)}) copy-start(f32[8192]{0:T(1024)} %param.10) | copy-start | bytes 98308
  360.2 185.9 %copy-start.23 = (f32[2,256]{1,0:T(2,128)S(1)}, f32[2,256]{1,0:T(2,128)}, u32[]{:S(2)}) copy-start(f32[2,256]{1,0:T(2,128)} %get-tuple-element.30) | copy-start | bytes 6148
  360.2 220.3 %reduce-scatter.3.cloned.1.call-start = ((), (), s32[]{:S(2)}) async-start(), calls=%async_computation.7 | async-start | bytes 2621440 | tf_op jit(solution)/shard_map/reduce_scatter | solution.py:137
  545.1 139.3 %reduce-scatter.5.cloned.1.call-start = ((), (), s32[]{:S(2)}) async-start(), calls=%async_computation.8 | async-start | bytes 10485760 | tf_op jit(solution)/shard_map/reduce_scatter | solution.py:149
  546.2 37.6 %copy-start.8 = (f32[2,256,256,4]{2,1,3,0:T(8,128)S(1)}, f32[2,256,256,4]{2,1,3,0:T(8,128)}, u32[]{:S(2)}) copy-start(f32[2,256,256,4]{2,1,3,0:T(8,128)} %copy-done.7) | copy-start | bytes 6291460
  583.7 7.0 slice-start.8
  585.4 4.1 copy-start.14
  585.4 5.3 slice-start.9
  745.9 14.9 %copy-start.3 = (f32[512,2048]{1,0:T(8,128)S(1)}, f32[512,2048]{1,0:T(8,128)}, u32[]{:S(2)}) copy-start(f32[512,2048]{1,0:T(8,128)} %copy-done.2) | copy-start | bytes 12582916
  745.9 17.6 %slice-start.4 = ((s8[16777216]{0:T(1024)(128)(4,1)}), s8[4194304]{0:T(1024)(128)(4,1)S(1)}, s32[]{:S(2)}) async-start(s8[16777216]{0:T(1024)(128)(4,1)} %bitcast.142), calls=%async_computation.14 | async-start | bytes 8388608
  745.9 17.6 %slice-start.5 = ((s8[16777216]{0:T(1024)(128)(4,1)}), s8[4194304]{0:T(1024)(128)(4,1)S(1)}, s32[]{:S(2)}) async-start(s8[16777216]{0:T(1024)(128)(4,1)} %bitcast.142), calls=%async_computation.15 | async-start | bytes 8388608
  746.0 17.6 %slice-start.6 = ((s8[16777216]{0:T(1024)(128)(4,1)}), s8[4194304]{0:T(1024)(128)(4,1)S(1)}, s32[]{:S(2)}) async-start(s8[16777216]{0:T(1024)(128)(4,1)} %bitcast.142), calls=%async_computation.16 | async-start | bytes 8388608
  764.2 7.6 copy-start.10
  764.2 10.6 %slice-start = ((s8[16777216]{0:T(1024)(128)(4,1)}), s8[4194304]{0:T(1024)(128)(4,1)S(1)}, s32[]{:S(2)}) async-start(s8[16777216]{0:T(1024)(128)(4,1)} %bitcast.140), calls=%async_computation.10 | async-start | bytes 8388608
  764.2 10.6 %slice-start.1 = ((s8[16777216]{0:T(1024)(128)(4,1)}), s8[4194304]{0:T(1024)(128)(4,1)S(1)}, s32[]{:S(2)}) async-start(s8[16777216]{0:T(1024)(128)(4,1)} %bitcast.140), calls=%async_computation.11 | async-start | bytes 8388608
  764.2 10.6 %slice-start.2 = ((s8[16777216]{0:T(1024)(128)(4,1)}), s8[4194304]{0:T(1024)(128)(4,1)S(1)}, s32[]{:S(2)}) async-start(s8[16777216]{0:T(1024)(128)(4,1)} %bitcast.140), calls=%async_computation.12 | async-start | bytes 8388608
  775.2 5.4 copy-start.5
  833.5 12.1 %copy-start.4 = (f32[512,2048]{1,0:T(8,128)S(1)}, f32[512,2048]{1,0:T(8,128)}, u32[]{:S(2)}) copy-start(f32[512,2048]{1,0:T(8,128)} %sub.60) | copy-start | bytes 12582916
  845.5 3.7 copy-start.6
  894.0 4.2 copy-start.9
  894.0 6.6 copy-start.1
  (11 other events, 23.4 us)
Sparse Core Ops, SparseCore 0:
  10.4 55.2 all-gather.6
  68.2 87.4 all-gather.14
  157.5 87.4 all-gather.8
  273.3 35.1 all-gather.12
  310.2 35.1 all-gather.10
  360.3 175.5 all-reduce.3
  545.2 35.2 reduce-scatter.2
  598.0 86.3 reduce-scatter.4
where the time goes:
time: 918 us; the launch traced here: 908 us
  waiting for transfers between devices  508 us (55%)
  other arithmetic  138 us (15%)
  blocking collectives  120 us (13%)
  matrix products  97.7 us (11%)
  local copies, waits for them, and re-layouts  26.5 us (3%)
  between operations  17.1 us (2%)
    psum x1, waiting for transfers between devices, body(): tangent_columns = lax.psum(group_term.astype(jnp.bfloat16), 'tensor')  176 us
    all_gather x1, waiting for transfers between devices, body(): lax.all_gather(dir_query, 'dp', axis=0, tiled=True)  81.5 us
    all_gather x1, waiting for transfers between devices, body(): lax.all_gather(q_weight, 'dp', axis=0, tiled=True)  76.5 us
    reduce_scatter x1, waiting for transfers between devices, body(): lax.psum_scatter((lax.dot_general(normed, cot_query, (((0,), (0,)), ((),...  58.9 us
    psum x1, blocking collectives, body(): lax.psum(local_products(kept_query, kept_output), ('dp', 'tensor'))  40.9 us
    psum x1, blocking collectives, body(): lax.psum(local_products(gn_query, gn_output), ('dp', 'tensor'))  39.5 us
    psum x1, blocking collectives, body(): squares = lax.psum(local_squares, ('dp', 'tensor')) / param_count  39.1 us
    all_gather x1, waiting for transfers between devices, body(): lax.all_gather(kv_pair, 'dp', axis=0, tiled=True)  34.5 us
  transfers between devices with their start and end apart: 8, of which 8 were waited for; matrix products, arithmetic and copies ran while one was open for 10% of the time, Pallas kernels for 0%

commit v1 on v0

--- a/solution.py
+++ b/solution.py
@@ -13,6 +13,24 @@
 ROPE_BASE = 500000.0
 NORM_EPS = 1e-05
 BETA_EPS = 1e-06
+
+
+def ring_gather(value, axis, dim):
+    ways, here, step = (lax.axis_size(axis), lax.axis_index(axis), value.shape[dim])
+    lengths = [n * ways if d == dim else n for d, n in enumerate(value.shape)]
+    full = lax.dynamic_update_slice_in_dim(
+        jnp.zeros(lengths, value.dtype), value, here * step, axis=dim
+    )
+    going_up = going_down = value
+    for far in range(1, ways // 2 + 1):
+        going_up = lax.ppermute(going_up, axis, [(d, (d + 1) % ways) for d in range(ways)])
+        full = lax.dynamic_update_slice_in_dim(full, going_up, (here - far) % ways * step, axis=dim)
+        if 2 * far < ways:
+            going_down = lax.ppermute(going_down, axis, [(d, (d - 1) % ways) for d in range(ways)])
+            full = lax.dynamic_update_slice_in_dim(
+                full, going_down, (here + far) % ways * step, axis=dim
+            )
+    return full
 
 
 def rope_tables(length, head_width):
@@ -95,11 +113,7 @@
     kv_head = lax.axis_index("tensor") * heads_dev // group_size
     kv_columns = lax.dynamic_slice_in_dim(kv_weight, kv_head * HD, HD, 2)
     kv_pair = jnp.concatenate([kv_columns[0], kv_columns[1]], axis=1)
-    sum_query = jnp.dot(
-        normed,
-        lax.all_gather(q_weight, "dp", axis=0, tiled=True),
-        preferred_element_type=jnp.float32,
-    )
+    sum_query = jnp.dot(normed, ring_gather(q_weight, "dp", 0), preferred_element_type=jnp.float32)
     sum_tangent = jnp.dot(
         normed,
         lax.all_gather(dir_query, "dp", axis=0, tiled=True),

time: 918 us -> 940 us (1.024)
  local copies, waits for them, and re-layouts: 26.5 us -> 39.7 us
    ppermute x0 -> x3, waiting for transfers between devices: none -> 196 us  [the longest x2 143 us: ring_gather(): lax.ppermute(going_up, axis, [(d, (d + 1) % ways) for d in range(ways)])]
    all_gather x1, waiting for transfers between devices: 81.5 us -> 0.01 us  [body(): lax.all_gather(dir_query, 'dp', axis=0, tiled=True)]
    all_gather x1 -> x0, waiting for transfers between devices: 76.5 us -> none  [body(): lax.all_gather(q_weight, 'dp', axis=0, tiled=True)]
    all_gather x1, waiting for transfers between devices: 34.5 us -> 0.02 us  [body(): lax.all_gather(kv_pair, 'dp', axis=0, tiled=True)]
    dynamic_update_slice x0 -> x4, local copies, waits for them, and re-layouts: none -> 9.48 us  [the longest x2 4.98 us: ring_gather(): lax.dynamic_update_slice_in_dim(full, going_up, (here - far) % ways * ste...]
  transfers between devices with their start and end apart: 8 -> 10, of which waited for: 8 -> 8; matrix products, arithmetic and copies ran while one was open for 10% -> 11% of each run, Pallas kernels for 0% -> 0%
where the time goes in v1:
time: 940 us; the launch traced here: 931 us
  waiting for transfers between devices  514 us (55%)
  other arithmetic  139 us (15%)
  blocking collectives  119 us (13%)
  matrix products  94.9 us (10%)
  local copies, waits for them, and re-layouts  39.7 us (4%)
  between operations  17.1 us (2%)
    psum x1, waiting for transfers between devices, body(): tangent_columns = lax.psum(group_term.astype(jnp.bfloat16), 'tensor')  176 us
    ppermute x2, waiting for transfers between devices, ring_gather(): lax.ppermute(going_up, axis, [(d, (d + 1) % ways) for d in range(ways)])  143 us
    reduce_scatter x1, waiting for transfers between devices, body(): lax.psum_scatter((lax.dot_general(normed, cot_query, (((0,), (0,)), ((),...  58.9 us
    ppermute x1, waiting for transfers between devices, ring_gather(): lax.ppermute(going_down, axis, [(d, (d - 1) % ways) for d in range(ways)])  53.4 us
    psum x1, blocking collectives, body(): lax.psum(local_products(kept_query, kept_output), ('dp', 'tensor'))  41 us
    psum x1, blocking collectives, body(): lax.psum(local_products(gn_query, gn_output), ('dp', 'tensor'))  39.5 us
    psum x1, blocking collectives, body(): squares = lax.psum(local_squares, ('dp', 'tensor')) / param_count  39 us
    all_gather x1, waiting for transfers between devices, body(): lax.all_gather(tangent_heads, 'dp', axis=0, tiled=True)  31.4 us
  transfers between devices with their start and end apart: 10, of which 8 were waited for; matrix products, arithmetic and copies ran while one was open for 11% of the time, Pallas kernels for 0%

profile of v1, /device:TPU:0, one launch (start us, length us, event | category | flops | bytes accessed | tf_op | source)
XLA Modules:
  0.0 931.4 jit_solution(16765232784331547087)
XLA Ops:
  17.0 5.7 multiply_reduce_fusion
  30.7 65.1 %collective-permute-done = bf16[2048,512]{1,0:T(8,128)(2,1)} collective-permute-done((bf16[2048,512]{1,0:T(8,128)(2,1)}, bf16[2048,512]{1,0:T(8,128)(2,1)}, u32[]{:S(2)}, u32[]{:S(2)}) %collective-permute-start) | collective-permute-done | bytes 2097184 | tf_op jit(solution)/shard_map/ppermute | solution.py:26
  98.3 10.1 %fusion.9 = bf16[512,8192]{1,0:T(8,128)(2,1)} fusion(f32[8192]{0:T(1024)S(1)} %copy-done.20, f32[512]{0:T(512)S(1)} %bitcast.158, bf16[2,256,8192]{2,1,0:T(8,128)(2,1)} %param.8), kind=kLoop, calls=%fused_computation.18 | loop fusion | flops 16777216 | bytes 16812032 | tf_op jit(solution)/shard_map/convert_element_type | solution.py:84
  112.0 53.4 %collective-permute-done.1 = bf16[2048,512]{1,0:T(8,128)(2,1)} collective-permute-done((bf16[2048,512]{1,0:T(8,128)(2,1)}, bf16[2048,512]{1,0:T(8,128)(2,1)}, u32[]{:S(2)}, u32[]{:S(2)}) %collective-permute-start.1) | collective-permute-done | bytes 2097184 | tf_op jit(solution)/shard_map/ppermute | solution.py:29
  168.4 77.9 %collective-permute-done.2 = bf16[2048,512]{1,0:T(8,128)(2,1)S(1)} collective-permute-done((bf16[2048,512]{1,0:T(8,128)(2,1)}, bf16[2048,512]{1,0:T(8,128)(2,1)S(1)}, u32[]{:S(2)}, u32[]{:S(2)}) %collective-permute-start.2) | collective-permute-done | bytes 2097184 | tf_op jit(solution)/shard_map/ppermute | solution.py:26
  247.8 8.1 fusion.47
  257.5 6.9 convolution_convert_fusion.2
  266.0 11.2 %fusion.44 = f32[512,512]{1,0:T(8,128)} fusion(bf16[512,8192]{1,0:T(8,128)(2,1)} %fusion.9, bf16[1,8192,512]{2,1,0:T(8,128)(2,1)} %all-gather.12.cloned.1.call-done), kind=kOutput, calls=%fused_computation.59 | convolution fusion | flops 4295753728 | bytes 17825792 | tf_op jit(solution)/shard_map/dot_general | solution.py:117
  300.4 31.4 %all-gather.10.cloned.1.call-done = bf16[2048,512]{1,0:T(8,128)(2,1)} async-done(((bf16[512,512]{1,0:T(8,128)(2,1)}), bf16[2048,512]{1,0:T(8,128)(2,1)}) %all-gather.10.cloned.1.call-update) | async-done | bytes 2097168 | tf_op jit(solution)/shard_map/all_gather | solution.py:145
  331.8 9.9 %fusion.95 = f32[2048,2048]{1,0:T(8,128)} fusion(bf16[2048,512]{1,0:T(8,128)(2,1)} %all-gather.10.cloned.1.call-done, bf16[512,2048]{1,0:T(8,128)(2,1)S(1)} %copy-done), kind=kOutput, calls=%fused_computation.138 | convolution fusion | flops 4294967296 | bytes 20971520 | tf_op jit(solution)/shard_map/dot_general | solution.py:149
  341.7 27.0 %all-gather.8.cloned.1.call-done = bf16[2048,512]{1,0:T(8,128)(2,1)} async-done(((bf16[512,512]{1,0:T(8,128)(2,1)}), bf16[2048,512]{1,0:T(8,128)(2,1)}) %all-gather.8.cloned.1.call-update) | async-done | bytes 2097168 | tf_op jit(solution)/shard_map/all_gather | solution.py:144
  368.7 14.8 %add_convert_fusion = bf16[2048,2048]{1,0:T(8,128)(2,1)} fusion(f32[2048,2048]{1,0:T(8,128)} %fusion.95, bf16[2048,512]{1,0:T(8,128)(2,1)} %all-gather.8.cloned.1.call-done, bf16[8,512,2048]{2,1,0:T(8,128)(2,1)} %param.15), kind=kOutput, calls=%fused_computation.22 | convolution fusion | flops 4307550208 | bytes 29360128 | tf_op jit(solution)/shard_map/dot_general | solution.py:147
  383.7 175.6 %all-reduce.4.cloned.1.call-done = bf16[2048,2048]{1,0:T(8,128)(2,1)} async-done(((bf16[2048,2048]{1,0:T(8,128)(2,1)}), bf16[2048,2048]{1,0:T(8,128)(2,1)}) %all-reduce.4.cloned.1.call-update) | async-done | bytes 8388624 | tf_op jit(solution)/shard_map/psum | solution.py:150
  559.3 9.3 convolution_convert_fusion
  569.5 10.0 %multiply_convert_fusion.2 = bf16[2,256,8192]{2,1,0:T(8,128)(2,1)} fusion(f32[8192]{0:T(1024)S(1)} %copy-done.21, f32[2,256]{1,0:T(2,128)S(1)} %copy-done.25, bf16[2,256,8192]{2,1,0:T(8,128)(2,1)} %param.8), kind=kLoop, calls=%fused_computation.23 | loop fusion | flops 16777216 | bytes 16812032 | tf_op jit(solution)/shard_map/convert_element_type | solution.py:84
  579.5 24.5 %reduce-scatter.3.cloned.1.call-done = bf16[512,512]{1,0:T(8,128)(2,1)} async-done(((bf16[2048,512]{1,0:T(8,128)(2,1)}), bf16[512,512]{1,0:T(8,128)(2,1)}) %reduce-scatter.3.cloned.1.call-update) | async-done | bytes 524304 | tf_op jit(solution)/shard_map/reduce_scatter | solution.py:151
  614.3 7.1 multiply_convert_fusion.1
  623.0 10.2 %multiply_convert_fusion = bf16[4,512,2048]{2,1,0:T(8,128)(2,1)} fusion(bf16[4,512,512]{2,1,0:T(8,128)(2,1)S(1)} %bitcast.160, bf16[4,512,2048]{2,1,0:T(8,128)(2,1)} %bitcast.159), kind=kOutput, calls=%fused_computation.20 | convolution fusion | flops 4303355904 | bytes 18874368 | tf_op jit(solution)/shard_map/nta,ntb->nab/dot_general | solution.py:91
  633.2 5.9 convert_reduce_fusion
  641.1 7.8 fusion.4
  649.0 58.9 %reduce-scatter.5.cloned.1.call-done = bf16[2048,512]{1,0:T(8,128)(2,1)} async-done(((bf16[8192,512]{1,0:T(8,128)(2,1)}), bf16[2048,512]{1,0:T(8,128)(2,1)}) %reduce-scatter.5.cloned.1.call-update) | async-done | bytes 2097168 | tf_op jit(solution)/shard_map/reduce_scatter | solution.py:163
  710.1 8.0 fusion
  718.0 39.5 %psum.29 = f32[8]{0:T(128)S(1)} all-reduce(f32[8]{0:T(128)S(1)} %add.104), channel_id=1, replica_groups=mesh['dp'=4,'tensor'=8] {'dp','tensor'}, use_global_device_ids=true, to_apply=%region_11.12 | all-reduce | flops 8 | bytes 64 | tf_op jit(solution)/shard_map/psum | solution.py:188
  757.5 11.9 %fusion.5 = f32[512,2048]{1,0:T(8,128)S(1)} fusion(bf16[8,512,2048]{2,1,0:T(8,128)(2,1)} %param.15, f32[8]{0:T(128)S(1)} %broadcast_multiply_fusion.1), kind=kLoop, calls=%fused_computation.13 | loop fusion | flops 24117248 | bytes 20971552 | tf_op jit(solution)/shard_map/reduce_sum | solution.py:185
  769.5 14.8 %fusion.1 = f32[2048,512]{1,0:T(8,128)} fusion(bf16[8,2048,512]{2,1,0:T(8,128)(2,1)} %param.14, f32[8]{0:T(128)S(1)} %broadcast_multiply_fusion.1), kind=kLoop, calls=%fused_computation.9 | loop fusion | flops 24117248 | bytes 20971552 | tf_op jit(solution)/shard_map/reduce_sum | solution.py:183
  787.7 7.6 fusion.6
  798.7 5.4 fusion.2
  804.1 41.0 %psum.30 = f32[8]{0:T(128)S(1)} all-reduce(f32[8]{0:T(128)S(1)} %add.105), channel_id=1, replica_groups=mesh['dp'=4,'tensor'=8] {'dp','tensor'}, use_global_device_ids=true, to_apply=%region_16.17 | all-reduce | flops 8 | bytes 64 | tf_op jit(solution)/shard_map/psum | solution.py:191
  845.1 11.9 %fusion.7 = f32[512,2048]{1,0:T(8,128)S(1)} fusion(bf16[8,512,2048]{2,1,0:T(8,128)(2,1)} %param.15, f32[8]{0:T(128)S(1)} %get-tuple-element.32), kind=kLoop, calls=%fused_computation.15 | loop fusion | flops 24117248 | bytes 20971552 | tf_op jit(solution)/shard_map/reduce_sum | solution.py:185
  857.0 12.1 %fusion.3 = f32[2048,512]{1,0:T(8,128)S(1)} fusion(bf16[8,2048,512]{2,1,0:T(8,128)(2,1)} %param.14, f32[8]{0:T(128)S(1)} %get-tuple-element.32), kind=kLoop, calls=%fused_computation.11 | loop fusion | flops 24117248 | bytes 20971552 | tf_op jit(solution)/shard_map/reduce_sum | solution.py:183
  877.7 39.0 %psum.31 = f32[]{:T(128)} all-reduce(f32[]{:T(128)S(6)} %add.106), channel_id=1, replica_groups=mesh['dp'=4,'tensor'=8] {'dp','tensor'}, use_global_device_ids=true, to_apply=%region_21.22 | all-reduce | flops 1 | bytes 8 | tf_op jit(solution)/shard_map/psum | solution.py:195
  917.5 4.1 divide_convert_fusion
  (147 shorter events, 88.0 us)
Async XLA Ops:
  7.2 324.7 %copy-start = (bf16[512,2048]{1,0:T(8,128)(2,1)S(1)}, bf16[512,2048]{1,0:T(8,128)(2,1)}, u32[]{:S(2)}) copy-start(bf16[512,2048]{1,0:T(8,128)(2,1)} %param.13) | copy-start | bytes 6291460
  7.2 250.3 %all-gather.6.cloned.1.call-start = ((), (), s32[]{:S(2)}) async-start(), calls=%async_computation.2 | async-start | bytes 5242880 | tf_op jit(solution)/shard_map/all_gather | solution.py:124
  9.8 256.2 %all-gather.12.cloned.1.call-start = ((), (), s32[]{:S(2)}) async-start(), calls=%async_computation.8 | async-start | bytes 10485760 | tf_op jit(solution)/shard_map/all_gather | solution.py:119
  12.9 318.9 %all-gather.10.cloned.1.call-start = ((), (), s32[]{:S(2)}) async-start(), calls=%async_computation.4 | async-start | bytes 2621440 | tf_op jit(solution)/shard_map/all_gather | solution.py:145
  13.0 82.9 %collective-permute-start = (bf16[2048,512]{1,0:T(8,128)(2,1)}, bf16[2048,512]{1,0:T(8,128)(2,1)}, u32[]{:S(2)}, u32[]{:S(2)}) collective-permute-start(bf16[2048,512]{1,0:T(8,128)(2,1)} %param.11), channel_id=1, source_target_pairs={{0,8},{8,16},{16,24},{24,0},{1,9},{9,17},{17,25},{25,1},{2,10},{10... | collective-permute-start | bytes 6291464 | tf_op jit(solution)/shard_map/ppermute | solution.py:26
  16.0 149.4 %collective-permute-start.1 = (bf16[2048,512]{1,0:T(8,128)(2,1)}, bf16[2048,512]{1,0:T(8,128)(2,1)}, u32[]{:S(2)}, u32[]{:S(2)}) collective-permute-start(bf16[2048,512]{1,0:T(8,128)(2,1)} %param.11), channel_id=1, source_target_pairs={{0,24},{8,0},{16,8},{24,16},{1,25},{9,1},{17,9},{25,17},{2,26},{10... | collective-permute-start | bytes 6291464 | tf_op jit(solution)/shard_map/ppermute | solution.py:29
  17.0 7.5 copy-start.24
  29.3 69.1 %copy-start.20 = (f32[8192]{0:T(1024)S(1)}, f32[8192]{0:T(1024)}, u32[]{:S(2)}) copy-start(f32[8192]{0:T(1024)} %param.10) | copy-start | bytes 98308
  95.9 150.5 %collective-permute-start.2 = (bf16[2048,512]{1,0:T(8,128)(2,1)}, bf16[2048,512]{1,0:T(8,128)(2,1)S(1)}, u32[]{:S(2)}, u32[]{:S(2)}) collective-permute-start(bf16[2048,512]{1,0:T(8,128)(2,1)} %collective-permute-done), channel_id=1, source_target_pairs={{0,8},{8,16},{16,24},{24,0},{1,9},{9,17},{17,25},{25,1},{2,10},{10... | collective-permute-start | bytes 6291464 | tf_op jit(solution)/shard_map/ppermute | solution.py:26
  112.0 135.9 %copy-start.11 = (bf16[512,8192]{1,0:T(8,128)(2,1)S(1)}, bf16[512,8192]{1,0:T(8,128)(2,1)}, u32[]{:S(2)}) copy-start(bf16[512,8192]{1,0:T(8,128)(2,1)} %fusion.9) | copy-start | bytes 25165828
  257.5 7.6 copy-start.13
  294.3 74.4 %all-gather.8.cloned.1.call-start = ((), (), s32[]{:S(2)}) async-start(), calls=%async_computation.3 | async-start | bytes 2621440 | tf_op jit(solution)/shard_map/all_gather | solution.py:144
  300.4 258.9 %all-reduce.4.cloned.1.call-start = ((), (), s32[]{:S(2)}) async-start(), calls=%async_computation.5 | async-start | bytes 16777216 | tf_op jit(solution)/shard_map/psum | solution.py:150
  383.6 185.1 %copy-start.18 = (pred[2,256,256]{1,2,0:T(8,128)(4,1)S(1)}, pred[2,256,256]{1,2,0:T(8,128)(4,1)}, u32[]{:S(2)}) copy-start(pred[2,256,256]{1,2,0:T(8,128)(4,1)} %get-tuple-element.27) | copy-start | bytes 393220
  383.6 185.9 %copy-start.21 = (f32[8192]{0:T(1024)S(1)}, f32[8192]{0:T(1024)}, u32[]{:S(2)}) copy-start(f32[8192]{0:T(1024)} %param.10) | copy-start | bytes 98308
  383.6 185.9 %copy-start.25 = (f32[2,256]{1,0:T(2,128)S(1)}, f32[2,256]{1,0:T(2,128)}, u32[]{:S(2)}) copy-start(f32[2,256]{1,0:T(2,128)} %get-tuple-element.30) | copy-start | bytes 6148
  383.6 220.4 %reduce-scatter.3.cloned.1.call-start = ((), (), s32[]{:S(2)}) async-start(), calls=%async_computation.6 | async-start | bytes 2621440 | tf_op jit(solution)/shard_map/reduce_scatter | solution.py:151
  568.6 139.3 %reduce-scatter.5.cloned.1.call-start = ((), (), s32[]{:S(2)}) async-start(), calls=%async_computation.7 | async-start | bytes 10485760 | tf_op jit(solution)/shard_map/reduce_scatter | solution.py:163
  569.5 37.8 %copy-start.8 = (f32[2,256,256,4]{2,1,3,0:T(8,128)S(1)}, f32[2,256,256,4]{2,1,3,0:T(8,128)}, u32[]{:S(2)}) copy-start(f32[2,256,256,4]{2,1,3,0:T(8,128)} %copy-done.7) | copy-start | bytes 6291460
  607.3 7.0 slice-start.8
  609.0 5.3 slice-start.9
  769.5 14.8 %copy-start.3 = (f32[512,2048]{1,0:T(8,128)S(1)}, f32[512,2048]{1,0:T(8,128)}, u32[]{:S(2)}) copy-start(f32[512,2048]{1,0:T(8,128)} %copy-done.2) | copy-start | bytes 12582916
  769.5 17.6 %slice-start.4 = ((s8[16777216]{0:T(1024)(128)(4,1)}), s8[4194304]{0:T(1024)(128)(4,1)S(1)}, s32[]{:S(2)}) async-start(s8[16777216]{0:T(1024)(128)(4,1)} %bitcast.142), calls=%async_computation.13 | async-start | bytes 8388608
  769.5 17.6 %slice-start.5 = ((s8[16777216]{0:T(1024)(128)(4,1)}), s8[4194304]{0:T(1024)(128)(4,1)S(1)}, s32[]{:S(2)}) async-start(s8[16777216]{0:T(1024)(128)(4,1)} %bitcast.142), calls=%async_computation.14 | async-start | bytes 8388608
  769.5 17.6 %slice-start.6 = ((s8[16777216]{0:T(1024)(128)(4,1)}), s8[4194304]{0:T(1024)(128)(4,1)S(1)}, s32[]{:S(2)}) async-start(s8[16777216]{0:T(1024)(128)(4,1)} %bitcast.142), calls=%async_computation.15 | async-start | bytes 8388608
  787.7 7.6 copy-start.10
  787.7 10.6 %slice-start = ((s8[16777216]{0:T(1024)(128)(4,1)}), s8[4194304]{0:T(1024)(128)(4,1)S(1)}, s32[]{:S(2)}) async-start(s8[16777216]{0:T(1024)(128)(4,1)} %bitcast.140), calls=%async_computation.9 | async-start | bytes 8388608
  787.7 10.6 %slice-start.1 = ((s8[16777216]{0:T(1024)(128)(4,1)}), s8[4194304]{0:T(1024)(128)(4,1)S(1)}, s32[]{:S(2)}) async-start(s8[16777216]{0:T(1024)(128)(4,1)} %bitcast.140), calls=%async_computation.10 | async-start | bytes 8388608
  787.7 10.6 %slice-start.2 = ((s8[16777216]{0:T(1024)(128)(4,1)}), s8[4194304]{0:T(1024)(128)(4,1)S(1)}, s32[]{:S(2)}) async-start(s8[16777216]{0:T(1024)(128)(4,1)} %bitcast.140), calls=%async_computation.11 | async-start | bytes 8388608
  798.7 5.4 copy-start.5
  857.0 12.1 %copy-start.4 = (f32[512,2048]{1,0:T(8,128)S(1)}, f32[512,2048]{1,0:T(8,128)}, u32[]{:S(2)}) copy-start(f32[512,2048]{1,0:T(8,128)} %sub.68) | copy-start | bytes 12582916
  917.5 6.6 copy-start.1
  (15 other events, 39.2 us)
Sparse Core Ops, SparseCore 0:
  9.9 88.6 all-gather.5
  101.1 153.2 all-gather.11
  294.5 37.3 all-gather.9
  333.5 35.1 all-gather.7
  383.7 175.5 all-reduce.3
  568.7 35.2 reduce-scatter.2
  621.5 86.3 reduce-scatter.4
